TPU v7x, 32 devices: a whole 2x2x4 slice. The times are simulated.
32 devices in a mesh: row: 8 (over z, core), col: 4 (over y, x).
Axes of the slice: x: 2, y: 2, z: 4, core: 2. Of those that a mesh axis runs over, the one named last changes fastest.
Arguments:
- inputs: bfloat16 [2, 64, 8192], P(None, None, 'col'), may hold values from -6 to 6
- w_input: bfloat16 [2, 4, 8192, 8192], P(None, None, 'row', 'col'), may hold values from -0.0625 to 0.0625
- w_recur: bfloat16 [2, 4, 8192, 8192], P(None, None, 'row', 'col'), may hold values from -0.0625 to 0.0625
- gate_bias: float32 [2, 4, 8192], P(None, None, 'row'), may hold values from -1 to 2
- hidden_init: bfloat16 [2, 64, 8192], P(None, None, ('row', 'col')), may hold values from -3 to 3
- cell_init: float32 [2, 64, 8192], P(None, None, ('row', 'col')), may hold values from -6 to 6
Outputs:
- top_hidden: bfloat16 [2, 64, 8192], P(None, None, ('row', 'col'))
- final_hidden: bfloat16 [2, 64, 8192], P(None, None, ('row', 'col'))
- final_cell: float32 [2, 64, 8192], P(None, None, ('row', 'col'))
All inputs are finite; a program needn't handle non-finite values.
Results may differ from a plain program's by a relative error of at most 0.009.
Values may be sent and summed in bfloat16 or wider, within the bound.
A program may use at most 128 MiB of HBM per device.

v0:
```python
import jax
import jax.numpy as jnp
from jax import lax
from jax.sharding import PartitionSpec as P


def lstm_cell(gate_total, cell_state):
    input_gate = jax.nn.sigmoid(gate_total[:, 0])
    forget_gate = jax.nn.sigmoid(gate_total[:, 1])
    candidate = jnp.tanh(gate_total[:, 2])
    output_gate = jax.nn.sigmoid(gate_total[:, 3])
    cell_state = forget_gate * cell_state + input_gate * candidate
    return (cell_state, (output_gate * jnp.tanh(cell_state)).astype(jnp.bfloat16))


def body(inputs, w_input, w_recur, gate_bias, hidden_init, cell_init):
    col_place = lax.axis_index("col")
    unit_width = hidden_init.shape[2]
    layers = w_input.shape[0]
    block_rows = w_input.shape[2]

    def project(vectors, weight):
        leading = vectors.shape[:-1]
        flattened = vectors.reshape(-1, vectors.shape[-1])
        result = lax.dot_general(
            flattened,
            weight.reshape(-1, weight.shape[-1]),
            (((1,), (1,)), ((), ())),
            preferred_element_type=jnp.float32,
        )
        return result.reshape(leading + (4, block_rows))

    def to_columns(owned):
        return lax.all_gather(owned, "row", axis=1, tiled=True)

    def gate_sums(partial_value, layer):
        bias_part = lax.dynamic_slice_in_dim(
            gate_bias[layer], col_place * unit_width, unit_width, 1
        )
        return (
            lax.psum_scatter(
                partial_value.astype(jnp.bfloat16), "col", scatter_dimension=2, tiled=True
            ).astype(jnp.float32)
            + bias_part[None]
        )

    def step_terms(layer, step_item):
        return project(step_item, w_input[layer])

    def advance(layer, lower_part, columns, cell_state):
        partial_value = lower_part + project(columns, w_recur[layer])
        cell_state, hidden = lstm_cell(gate_sums(partial_value, layer), cell_state)
        return (hidden, to_columns(hidden), cell_state)

    start_columns = tuple((to_columns(hidden_init[layer]) for layer in range(layers)))
    start_owned = tuple((hidden_init[layer] for layer in range(layers)))
    start_state = tuple((cell_init[layer] for layer in range(layers)))

    def advance_time(carried, step_item):
        owned_all, columns_all, cells_all = carried
        next_owned, next_columns, next_cells = ([], [], [])
        lower_part = step_terms(0, step_item)
        for layer in range(layers):
            if layer > 0:
                lower_part = project(next_columns[layer - 1], w_input[layer])
            owned, columns, cell_state = advance(
                layer, lower_part, columns_all[layer], cells_all[layer]
            )
            next_owned.append(owned)
            next_columns.append(columns)
            next_cells.append(cell_state)
        return ((tuple(next_owned), tuple(next_columns), tuple(next_cells)), next_owned[-1])

    carried, top_hidden = lax.scan(advance_time, (start_owned, start_columns, start_state), inputs)
    final_owned, final_columns, final_cells = carried
    final_hidden = jnp.stack(final_owned)
    final_cell = jnp.stack(final_cells)
    return (top_hidden, final_hidden, final_cell)


def solution(mesh):
    in_specs = (
        P(None, None, "col"),
        P(None, None, "row", "col"),
        P(None, None, "row", "col"),
        P(None, None, "row"),
        P(None, None, ("row", "col")),
        P(None, None, ("row", "col")),
    )
    out_specs = (
        P(None, None, ("row", "col")),
        P(None, None, ("row", "col")),
        P(None, None, ("row", "col")),
    )
    return jax.shard_map(body, mesh=mesh, in_specs=in_specs, out_specs=out_specs, check_vma=False)
```

profile of v0, /device:TPU:0, one launch (start us, length us, event | category | flops | bytes accessed | tf_op | source)
XLA Modules:
  0.0 273.1 jit_solution(4128591278328970384)
XLA Ops:
  7.9 1.4 fusion.67
  9.3 15.9 %all-gather = bf16[1,64,2048]{2,1,0:T(8,128)(2,1)S(1)} all-gather(bf16[1,64,256]{2,1,0:T(8,128)(2,1)S(1)} %get-tuple-element.197), channel_id=2, replica_groups=mesh['row'=8,'col'=4] {'row'}, dimensions={2}, use_global_device_ids=true | all-gather | bytes 294912 | tf_op jit(solution)/shard_map/all_gather | solution.py:34
  25.2 14.2 %all-gather.1 = bf16[1,64,2048]{2,1,0:T(8,128)(2,1)S(1)} all-gather(bf16[1,64,256]{2,1,0:T(8,128)(2,1)S(1)} %get-tuple-element.194), channel_id=3, replica_groups=mesh['row'=8,'col'=4] {'row'}, dimensions={2}, use_global_device_ids=true | all-gather | bytes 294912 | tf_op jit(solution)/shard_map/all_gather | solution.py:34
  40.3 224.2 %while.24 = (s32[]{:T(128)}, bf16[64,256]{1,0:T(8,128)(2,1)}, bf16[64,256]{1,0:T(8,128)(2,1)}, bf16[64,2048]{1,0:T(8,128)(2,1)S(1)}, bf16[64,2048]{1,0:T(8,128)(...) while((s32[]{:T(128)}, bf16[64,256]{1,0:T(8,128)(2,1)}, ...), condition=%wide.region_3.4_spmd, body=%wide.region_0.3_spmd.sunk | while | flops 4296736768 | bytes 79864096 | solution.py:74
  40.4 8.7 %fusion.90 = f32[64,4,1024]{2,0,1:T(8,128)S(1)} fusion(bf16[2,4,1024,2048]{3,2,1,0:T(8,128)(2,1)} %get-tuple-element.325, bf16[64,2048]{1,0:T(8,128)(2,1)S(1)} %get-tuple-element.304), kind=kOutput, calls=%fused_computation.4.clone.1 | convolution fusion | flops 1073741824 | bytes 18087936 | tf_op jit(solution)/shard_map/while/body/eval_jaxpr/dot_general | solution.py:25
  49.1 11.9 %fusion.91 = bf16[64,4,1024]{2,0,1:T(8,128)(2,1)} fusion(f32[64,4,1024]{2,0,1:T(8,128)S(1)} %fusion.90, bf16[2,4,1024,2048]{3,2,1,0:T(8,128)(2,1)} %get-tuple-element.324, bf16[2,64,2048]{2,1,0:T(8,128)(2,1)} %get-tuple-element.323, s32[]{:T(128)S(6)} %copy.18), kind=kOutput, calls=%fused_computation.15.clone.1 | convolution fusion | flops 1074266112 | bytes 18612228 | tf_op jit(solution)/shard_map/while/body/eval_jaxpr/dot_general | solution.py:25
  61.1 8.7 %fusion.93 = f32[64,4,1024]{2,0,1:T(8,128)S(1)} fusion(bf16[2,4,1024,2048]{3,2,1,0:T(8,128)(2,1)} %get-tuple-element.325, bf16[64,2048]{1,0:T(8,128)(2,1)S(1)} %get-tuple-element.305), kind=kOutput, calls=%fused_computation.clone.1 | convolution fusion | flops 1073741824 | bytes 18087936 | tf_op jit(solution)/shard_map/while/body/eval_jaxpr/dot_general | solution.py:25
  69.8 17.6 %reduce-scatter.3.cloned.1.call-done = bf16[64,4,256]{2,0,1:T(8,128)(2,1)} async-done(((bf16[64,4,1024]{2,0,1:T(8,128)(2,1)}), bf16[64,4,256]{2,0,1:T(8,128)(2,1)}) %reduce-scatter.3.cloned.1.call-update) | async-done | bytes 131088 | tf_op jit(solution)/shard_map/while/body/eval_jaxpr/reduce_scatter | solution.py:41
  87.4 0.9 convert_add_fusion.4
  88.4 14.3 %all_gather.20 = bf16[64,2048]{1,0:T(8,128)(2,1)S(1)} all-gather(bf16[64,256]{1,0:T(8,128)(2,1)S(1)} %get-tuple-element.316), channel_id=1, replica_groups=mesh['row'=8,'col'=4] {'row'}, dimensions={1}, use_global_device_ids=true | all-gather | bytes 294912 | tf_op jit(solution)/shard_map/while/body/eval_jaxpr/all_gather | solution.py:34
  102.7 9.7 %fusion.94 = bf16[64,4,1024]{2,0,1:T(8,128)(2,1)} fusion(f32[64,4,1024]{2,0,1:T(8,128)S(1)} %fusion.93, bf16[2,4,1024,2048]{3,2,1,0:T(8,128)(2,1)} %get-tuple-element.324, bf16[64,2048]{1,0:T(8,128)(2,1)S(1)} %all_gather.20), kind=kOutput, calls=%fused_computation.14.clone.1 | convolution fusion | flops 1074266112 | bytes 18612224 | tf_op jit(solution)/shard_map/while/body/eval_jaxpr/dot_general | solution.py:25
  112.4 25.2 %reduce-scatter.5.cloned.1.call-done = bf16[64,4,256]{2,0,1:T(8,128)(2,1)} async-done(((bf16[64,4,1024]{2,0,1:T(8,128)(2,1)}), bf16[64,4,256]{2,0,1:T(8,128)(2,1)}) %reduce-scatter.5.cloned.1.call-update) | async-done | bytes 131088 | tf_op jit(solution)/shard_map/while/body/eval_jaxpr/reduce_scatter | solution.py:41
  138.7 14.3 %all_gather.21 = bf16[64,2048]{1,0:T(8,128)(2,1)S(1)} all-gather(bf16[64,256]{1,0:T(8,128)(2,1)S(1)} %get-tuple-element.317), channel_id=1, replica_groups=mesh['row'=8,'col'=4] {'row'}, dimensions={1}, use_global_device_ids=true | all-gather | bytes 294912 | tf_op jit(solution)/shard_map/while/body/eval_jaxpr/all_gather | solution.py:34
  153.0 8.7 %fusion.90 = f32[64,4,1024]{2,0,1:T(8,128)S(1)} fusion(bf16[2,4,1024,2048]{3,2,1,0:T(8,128)(2,1)} %get-tuple-element.325, bf16[64,2048]{1,0:T(8,128)(2,1)S(1)} %get-tuple-element.304), kind=kOutput, calls=%fused_computation.4.clone.1 | convolution fusion | flops 1073741824 | bytes 18087936 | tf_op jit(solution)/shard_map/while/body/eval_jaxpr/dot_general | solution.py:25
  161.7 11.9 %fusion.91 = bf16[64,4,1024]{2,0,1:T(8,128)(2,1)} fusion(f32[64,4,1024]{2,0,1:T(8,128)S(1)} %fusion.90, bf16[2,4,1024,2048]{3,2,1,0:T(8,128)(2,1)} %get-tuple-element.324, bf16[2,64,2048]{2,1,0:T(8,128)(2,1)} %get-tuple-element.323, s32[]{:T(128)S(6)} %copy.18), kind=kOutput, calls=%fused_computation.15.clone.1 | convolution fusion | flops 1074266112 | bytes 18612228 | tf_op jit(solution)/shard_map/while/body/eval_jaxpr/dot_general | solution.py:25
  173.7 8.7 %fusion.93 = f32[64,4,1024]{2,0,1:T(8,128)S(1)} fusion(bf16[2,4,1024,2048]{3,2,1,0:T(8,128)(2,1)} %get-tuple-element.325, bf16[64,2048]{1,0:T(8,128)(2,1)S(1)} %get-tuple-element.305), kind=kOutput, calls=%fused_computation.clone.1 | convolution fusion | flops 1073741824 | bytes 18087936 | tf_op jit(solution)/shard_map/while/body/eval_jaxpr/dot_general | solution.py:25
  182.4 16.5 %reduce-scatter.3.cloned.1.call-done = bf16[64,4,256]{2,0,1:T(8,128)(2,1)} async-done(((bf16[64,4,1024]{2,0,1:T(8,128)(2,1)}), bf16[64,4,256]{2,0,1:T(8,128)(2,1)}) %reduce-scatter.3.cloned.1.call-update) | async-done | bytes 131088 | tf_op jit(solution)/shard_map/while/body/eval_jaxpr/reduce_scatter | solution.py:41
  198.9 0.9 convert_add_fusion.4
  199.9 14.3 %all_gather.20 = bf16[64,2048]{1,0:T(8,128)(2,1)S(1)} all-gather(bf16[64,256]{1,0:T(8,128)(2,1)S(1)} %get-tuple-element.316), channel_id=1, replica_groups=mesh['row'=8,'col'=4] {'row'}, dimensions={1}, use_global_device_ids=true | all-gather | bytes 294912 | tf_op jit(solution)/shard_map/while/body/eval_jaxpr/all_gather | solution.py:34
  214.2 9.7 %fusion.94 = bf16[64,4,1024]{2,0,1:T(8,128)(2,1)} fusion(f32[64,4,1024]{2,0,1:T(8,128)S(1)} %fusion.93, bf16[2,4,1024,2048]{3,2,1,0:T(8,128)(2,1)} %get-tuple-element.324, bf16[64,2048]{1,0:T(8,128)(2,1)S(1)} %all_gather.20), kind=kOutput, calls=%fused_computation.14.clone.1 | convolution fusion | flops 1074266112 | bytes 18612224 | tf_op jit(solution)/shard_map/while/body/eval_jaxpr/dot_general | solution.py:25
  223.9 25.3 %reduce-scatter.5.cloned.1.call-done = bf16[64,4,256]{2,0,1:T(8,128)(2,1)} async-done(((bf16[64,4,1024]{2,0,1:T(8,128)(2,1)}), bf16[64,4,256]{2,0,1:T(8,128)(2,1)}) %reduce-scatter.5.cloned.1.call-update) | async-done | bytes 131088 | tf_op jit(solution)/shard_map/while/body/eval_jaxpr/reduce_scatter | solution.py:41
  249.1 0.9 convert_add_fusion.5
  250.2 14.3 %all_gather.21 = bf16[64,2048]{1,0:T(8,128)(2,1)S(1)} all-gather(bf16[64,256]{1,0:T(8,128)(2,1)S(1)} %get-tuple-element.317), channel_id=1, replica_groups=mesh['row'=8,'col'=4] {'row'}, dimensions={1}, use_global_device_ids=true | all-gather | bytes 294912 | tf_op jit(solution)/shard_map/while/body/eval_jaxpr/all_gather | solution.py:34
  265.2 1.4 pad_maximum_fusion.1
  (28 shorter events, 3.8 us)
Async XLA Ops:
  40.3 47.1 %reduce-scatter.3.cloned.1.call-start = ((), (), s32[]{:S(2)}) async-start(), calls=%async_computation.2 | async-start | bytes 655360 | tf_op jit(solution)/shard_map/while/body/eval_jaxpr/reduce_scatter | solution.py:41
  61.0 76.6 %reduce-scatter.5.cloned.1.call-start = ((), (), s32[]{:S(2)}) async-start(), calls=%async_computation.3 | async-start | bytes 655360 | tf_op jit(solution)/shard_map/while/body/eval_jaxpr/reduce_scatter | solution.py:41
  88.4 64.6 %copy-start = (bf16[64,256]{1,0:T(8,128)(2,1)}, bf16[64,256]{1,0:T(8,128)(2,1)S(1)}, u32[]{:S(2)}) copy-start(bf16[64,256]{1,0:T(8,128)(2,1)S(1)} %get-tuple-element.316) | copy-start | bytes 98308 | tf_op jit(solution)/shard_map/while
  138.6 14.3 %copy-start.1 = (bf16[64,256]{1,0:T(8,128)(2,1)}, bf16[64,256]{1,0:T(8,128)(2,1)S(1)}, u32[]{:S(2)}) copy-start(bf16[64,256]{1,0:T(8,128)(2,1)S(1)} %get-tuple-element.317) | copy-start | bytes 98308 | tf_op jit(solution)/shard_map/while
  153.0 45.9 %reduce-scatter.3.cloned.1.call-start = ((), (), s32[]{:S(2)}) async-start(), calls=%async_computation.2 | async-start | bytes 655360 | tf_op jit(solution)/shard_map/while/body/eval_jaxpr/reduce_scatter | solution.py:41
  173.6 75.5 %reduce-scatter.5.cloned.1.call-start = ((), (), s32[]{:S(2)}) async-start(), calls=%async_computation.3 | async-start | bytes 655360 | tf_op jit(solution)/shard_map/while/body/eval_jaxpr/reduce_scatter | solution.py:41
  199.9 64.6 %copy-start = (bf16[64,256]{1,0:T(8,128)(2,1)}, bf16[64,256]{1,0:T(8,128)(2,1)S(1)}, u32[]{:S(2)}) copy-start(bf16[64,256]{1,0:T(8,128)(2,1)S(1)} %get-tuple-element.316) | copy-start | bytes 98308 | tf_op jit(solution)/shard_map/while
  250.2 14.3 %copy-start.1 = (bf16[64,256]{1,0:T(8,128)(2,1)}, bf16[64,256]{1,0:T(8,128)(2,1)S(1)}, u32[]{:S(2)}) copy-start(bf16[64,256]{1,0:T(8,128)(2,1)S(1)} %get-tuple-element.317) | copy-start | bytes 98308 | tf_op jit(solution)/shard_map/while
  264.5 2.1 copy-start.2
Sparse Core Ops, SparseCore 0:
  61.1 26.2 reduce-scatter.2
  112.6 25.0 reduce-scatter.4
  173.7 25.0 reduce-scatter.2
  224.0 25.1 reduce-scatter.4
where the time goes:
time: 274 us; the launch traced here: 273 us
  blocking collectives  87.3 us (32%)
  waiting for transfers between devices  84.6 us (31%)
  matrix products  78.1 us (29%)
  between operations  13.7 us (5%)
  other arithmetic  6.13 us (2%)
  local copies, waits for them, and re-layouts  3.06 us (1%)
    all_gather x6, blocking collectives, to_columns(): return lax.all_gather(owned, 'row', axis=1, tiled=True)  87.3 us
    reduce_scatter x4, waiting for transfers between devices, gate_sums(): lax.psum_scatter(partial_value.astype(jnp.bfloat16), 'col', scatter_dimen...  84.5 us
    dot_general x8, matrix products, project(): lax.dot_general(flattened, weight.reshape(-1, weight.shape[-1]), (((1,),...  78.1 us
  transfers between devices with their start and end apart: 4, of which 4 were waited for; matrix products, arithmetic and copies ran while one was open for 6% of the time, Pallas kernels for 0%

commit v1 on v0

v1 whole, which is shorter than its diff:
```python
import functools

import jax
import jax.numpy as jnp
from jax import lax
from jax.experimental import pallas as pl
from jax.experimental.pallas import tpu as pltpu
from jax.sharding import PartitionSpec as P

MESH = pl.DeviceIdType.MESH
GATES = 4
LOCAL_VMEM = 67_043_328


def lstm_cell(gate_total, cell_state):
    input_gate = jax.nn.sigmoid(gate_total[:, 0])
    forget_gate = jax.nn.sigmoid(gate_total[:, 1])
    candidate = jnp.tanh(gate_total[:, 2])
    output_gate = jax.nn.sigmoid(gate_total[:, 3])
    cell_state = forget_gate * cell_state + input_gate * candidate
    return (cell_state, (output_gate * jnp.tanh(cell_state)).astype(jnp.bfloat16))


def general_body(inputs, w_input, w_recur, gate_bias, hidden_init, cell_init):
    col_place = lax.axis_index("col")
    unit_width = hidden_init.shape[2]
    layers = w_input.shape[0]
    block_rows = w_input.shape[2]

    def project(vectors, weight):
        result = lax.dot_general(
            vectors,
            weight.reshape(-1, weight.shape[-1]),
            (((1,), (1,)), ((), ())),
            preferred_element_type=jnp.float32,
        )
        return result.reshape(vectors.shape[:-1] + (GATES, block_rows))

    def to_columns(owned):
        return lax.all_gather(owned, "row", axis=1, tiled=True)

    def gate_sums(partial_value, layer):
        bias_part = lax.dynamic_slice_in_dim(
            gate_bias[layer], col_place * unit_width, unit_width, 1
        )
        return (
            lax.psum_scatter(
                partial_value.astype(jnp.bfloat16), "col", scatter_dimension=2, tiled=True
            ).astype(jnp.float32)
            + bias_part[None]
        )

    start = tuple(
        (hidden_init[layer], to_columns(hidden_init[layer]), cell_init[layer])
        for layer in range(layers)
    )

    def advance_time(carried, step_item):
        lower, following = step_item, []
        for layer in range(layers):
            _, columns, cell_state = carried[layer]
            partial_value = project(lower, w_input[layer]) + project(columns, w_recur[layer])
            cell_state, owned = lstm_cell(gate_sums(partial_value, layer), cell_state)
            lower = to_columns(owned)
            following.append((owned, lower, cell_state))
        return tuple(following), following[-1][0]

    carried, top_hidden = lax.scan(advance_time, start, inputs)
    return (
        top_hidden,
        jnp.stack([item[0] for item in carried]),
        jnp.stack([item[2] for item in carried]),
    )


def xor(value, mask, size):
    total, bit = 0, 1
    while bit < size:
        total = total + bit * ((value // bit + mask // bit) % 2)
        bit *= 2
    return total


def window_kernel(
    n_row, n_col,
    inputs, w_input, w_recur, gate_bias, hidden_init, cell_init,
    top_hidden, final_hidden, final_cell,
    first, second, third, sums, sent, arrived, columns,
    first_sem, first_again_sem, second_sem, third_sem,
    part_send, part_recv, block_send, block_recv,
):
    row, col = lax.axis_index("row"), lax.axis_index("col")
    unit = hidden_init.shape[2]
    batch = hidden_init.shape[1]
    chips = n_row // 2
    last = n_col - 1
    sibling = row + 1 - 2 * (row % 2)

    def owner_of(i):
        return xor(col, last - i, n_col)

    def load(weight, layer, buffer, sems, i, g):
        start = pl.multiple_of(owner_of(i) * unit, unit)
        k = i * GATES + g
        return pltpu.make_async_copy(
            weight.at[layer, g, pl.ds(start, unit), :], buffer.at[k], sems.at[k]
        )

    def far(k):
        return (row + 2 * k) % n_row

    def near(k):
        return (row + n_row - 2 * k) % n_row

    def send_block(which, source, owner, target, slot):
        return pltpu.make_async_remote_copy(
            src_ref=source,
            dst_ref=columns.at[which, owner],
            send_sem=block_send.at[which, slot],
            recv_sem=block_recv.at[which, slot],
            device_id=(target, col),
            device_id_type=MESH,
        )

    def gather_start(which, source):
        for k in range(1, chips):
            send_block(which, source, row, far(k), k).start()
        send_block(which, source, row, sibling, 0).start()

    def gather_forward(which):
        for k in range(1, chips):
            owner = near(k)
            send_block(which, columns.at[which, owner], owner, far(k), k).wait_recv()
            send_block(
                which, columns.at[which, owner], owner, sibling, chips - 1 + k
            ).start()

    def gather_wait(which):
        block = columns.at[which, sibling]
        send_block(which, block, sibling, sibling, 0).wait_recv()
        for k in range(1, chips):
            block = columns.at[which, (sibling + n_row - 2 * k) % n_row]
            send_block(which, block, row, sibling, chips - 1 + k).wait_recv()

    def gather_end(which):
        for slot in range(2 * chips - 1):
            send_block(which, columns.at[which, row], row, sibling, slot).wait_send()

    def vectors(which):
        return jnp.concatenate([columns[which, r] for r in range(n_row)], axis=1)

    def product(left, buffer, k):
        return lax.dot_general(
            left, buffer[k], (((1,), (1,)), ((), ())), preferred_element_type=jnp.float32
        )

    def send_part(which, i):
        return pltpu.make_async_remote_copy(
            src_ref=sent.at[which, i],
            dst_ref=arrived.at[which, i],
            send_sem=part_send.at[which, i],
            recv_sem=part_recv.at[which, i],
            device_id=(row, owner_of(i)),
            device_id_type=MESH,
        )

    def finish(which, held, buffer, i, before=None):
        left = vectors(held)
        totals = []
        for g in range(GATES):
            if before is not None:
                before(i, g)
            k = i * GATES + g
            totals.append(sums[which, k] + product(left, buffer, k))

        @pl.when(i < last)
        def _():
            for g in range(GATES):
                sent[which, i, g] = totals[g].astype(jnp.bfloat16)
            send_part(which, i).start()

        @pl.when(i == last)
        def _():
            for g in range(GATES):
                sums[which, last * GATES + g] = totals[g]

    def cell_step(which, layer, old_cell):
        for i in range(last):
            send_part(which, i).wait_recv()
        totals = []
        for g in range(GATES):
            total = sums[which, last * GATES + g]
            for i in range(last):
                total = total + arrived[which, i, g].astype(jnp.float32)
            bias = gate_bias[layer, pl.ds(g, 1), pl.ds(pl.multiple_of(col * unit, unit), unit)]
            totals.append(total + bias)
        cell = jax.nn.sigmoid(totals[1]) * old_cell + jax.nn.sigmoid(totals[0]) * jnp.tanh(totals[2])
        hidden = (jax.nn.sigmoid(totals[3]) * jnp.tanh(cell)).astype(jnp.bfloat16)
        return cell, hidden

    def loop(begin, end, step):
        def run(i, carried):
            step(i)
            return carried
        lax.fori_loop(begin, end, run, 0)

    for i in range(n_col):
        for g in range(GATES):
            load(w_input, 0, first, first_sem, i, g).start()
    for i in range(n_col):
        for g in range(GATES):
            load(w_recur, 0, second, second_sem, i, g).start()

    barrier = pltpu.get_barrier_semaphore()
    targets = [(sibling, col)]
    targets += [(far(k), col) for k in range(1, chips)]
    targets += [(row, owner_of(i)) for i in range(last)]
    for target in targets:
        pl.semaphore_signal(barrier, inc=1, device_id=target, device_id_type=MESH)
    pl.semaphore_wait(barrier, len(targets))

    for layer in range(2):
        gather_start(layer, hidden_init.at[layer])
        columns[layer, row] = hidden_init[layer]

    def input_products(i):
        left = inputs[...].reshape(2 * batch, inputs.shape[2])
        for g in range(GATES):
            k = i * GATES + g
            load(w_input, 0, first, first_sem, i, g).wait()
            both = product(left, first, k)
            sums[0, k] = both[:batch]
            sums[1, k] = both[batch:]

    half = n_col // 2
    loop(0, half, input_products)
    gather_forward(0)
    loop(half, n_col, input_products)
    gather_forward(1)
    gather_wait(0)

    def layer0_step0(i):
        def before(i, g):
            load(w_recur, 0, second, second_sem, i, g).wait()
            load(w_recur, 1, first, first_again_sem, i, g).start()

        finish(0, 0, second, i, before)

    loop(0, n_col, layer0_step0)
    for i in range(n_col):
        for g in range(GATES):
            load(w_input, 1, third, third_sem, i, g).start()
    gather_wait(1)

    def early_recurrent(i):
        left = vectors(1)
        for g in range(GATES):
            k = i * GATES + g
            load(w_recur, 1, first, first_again_sem, i, g).wait()
            sums[2, k] = product(left, first, k)

    loop(0, half, early_recurrent)
    cell, hidden = cell_step(0, 0, cell_init[0])
    columns[2, row] = hidden
    gather_start(2, columns.at[2, row])
    final_cell[0] = cell
    loop(half, n_col, early_recurrent)
    gather_forward(2)
    gather_wait(2)

    loop(0, n_col, lambda i: finish(1, 2, second, i))

    def layer1_step0(i):
        finish(2, 2, third, i, lambda i, g: load(w_input, 1, third, third_sem, i, g).wait())

    loop(0, half, layer1_step0)
    cell, hidden = cell_step(1, 0, final_cell[0])
    columns[3, row] = hidden
    gather_start(3, columns.at[3, row])
    final_cell[0] = cell
    final_hidden[0] = hidden
    loop(half, n_col, layer1_step0)
    gather_forward(3)
    gather_wait(3)

    def late_input(i):
        left = vectors(3)
        for g in range(GATES):
            k = i * GATES + g
            sums[3, k] = product(left, third, k)

    loop(0, half, late_input)
    cell, hidden = cell_step(2, 1, cell_init[1])
    columns[4, row] = hidden
    gather_start(4, columns.at[4, row])
    final_cell[1] = cell
    top_hidden[0] = hidden
    loop(half, n_col, late_input)
    gather_forward(4)
    gather_wait(4)
    loop(0, n_col, lambda i: finish(3, 4, first, i))
    cell, hidden = cell_step(3, 1, final_cell[1])
    final_cell[1] = cell
    top_hidden[1] = hidden
    final_hidden[1] = hidden

    for which in range(5):
        gather_end(which)
    for which in range(4):
        for i in range(last):
            send_part(which, i).wait_send()


def window_body(n_row, n_col, inputs, w_input, w_recur, gate_bias, hidden_init, cell_init):
    batch, unit = hidden_init.shape[1:]
    depth = w_input.shape[3]
    chunks = n_col * GATES
    chips = n_row // 2
    vmem = pl.BlockSpec(memory_space=pltpu.VMEM)
    hbm = pl.BlockSpec(memory_space=pl.ANY)
    return pl.pallas_call(
        functools.partial(window_kernel, n_row, n_col),
        out_shape=(
            jax.ShapeDtypeStruct((2, batch, unit), jnp.bfloat16),
            jax.ShapeDtypeStruct((2, batch, unit), jnp.bfloat16),
            jax.ShapeDtypeStruct((2, batch, unit), jnp.float32),
        ),
        in_specs=[vmem, hbm, hbm, vmem, vmem, vmem],
        out_specs=(vmem, vmem, vmem),
        scratch_shapes=[
            pltpu.VMEM((chunks, unit, depth), jnp.bfloat16),
            pltpu.VMEM((chunks, unit, depth), jnp.bfloat16),
            pltpu.VMEM((chunks, unit, depth), jnp.bfloat16),
            pltpu.VMEM((4, chunks, batch, unit), jnp.float32),
            pltpu.VMEM((4, n_col - 1, GATES, batch, unit), jnp.bfloat16),
            pltpu.VMEM((4, n_col - 1, GATES, batch, unit), jnp.bfloat16),
            pltpu.VMEM((5, n_row, batch, unit), jnp.bfloat16),
            pltpu.SemaphoreType.DMA((chunks,)),
            pltpu.SemaphoreType.DMA((chunks,)),
            pltpu.SemaphoreType.DMA((chunks,)),
            pltpu.SemaphoreType.DMA((chunks,)),
            pltpu.SemaphoreType.DMA((4, n_col - 1)),
            pltpu.SemaphoreType.DMA((4, n_col - 1)),
            pltpu.SemaphoreType.DMA((5, 2 * chips - 1)),
            pltpu.SemaphoreType.DMA((5, 2 * chips - 1)),
        ],
        compiler_params=pltpu.CompilerParams(
            collective_id=0, has_side_effects=True, vmem_limit_bytes=LOCAL_VMEM
        ),
    )(inputs, w_input, w_recur, gate_bias, hidden_init, cell_init)


def solution(mesh):
    n_row, n_col = mesh.shape["row"], mesh.shape["col"]

    def body(inputs, w_input, w_recur, gate_bias, hidden_init, cell_init):
        unit = hidden_init.shape[2]
        held = 3 * w_input.size // w_input.shape[0] * 2
        fits = (
            inputs.shape[0] == 2
            and w_input.shape[0] == 2
            and unit % 128 == 0
            and n_row % 2 == 0
            and n_row >= 4
            and n_col >= 2
            and n_col & (n_col - 1) == 0
            and held + held // 4 < LOCAL_VMEM
        )
        args = (inputs, w_input, w_recur, gate_bias, hidden_init, cell_init)
        return window_body(n_row, n_col, *args) if fits else general_body(*args)

    in_specs = (
        P(None, None, "col"),
        P(None, None, "row", "col"),
        P(None, None, "row", "col"),
        P(None, None, "row"),
        P(None, None, ("row", "col")),
        P(None, None, ("row", "col")),
    )
    out_specs = (
        P(None, None, ("row", "col")),
        P(None, None, ("row", "col")),
        P(None, None, ("row", "col")),
    )
    return jax.shard_map(body, mesh=mesh, in_specs=in_specs, out_specs=out_specs, check_vma=False)
```

time: 274 us -> 83.6 us (0.31)
  blocking collectives: 87.3 us -> 0 us
  waiting for transfers between devices: 84.6 us -> 0 us
  Pallas kernels: 0 us -> 78.2 us
  matrix products: 78.1 us -> 0 us
  between operations: 13.7 us -> 0.64 us
  other arithmetic: 6.13 us -> 0 us
    all_gather x6 -> x0, blocking collectives: 87.3 us -> none  [to_columns(): return lax.all_gather(owned, 'row', axis=1, tiled=True)]
    reduce_scatter x4 -> x0, waiting for transfers between devices: 84.5 us -> none  [gate_sums(): lax.psum_scatter(partial_value.astype(jnp.bfloat16), 'col', scatter_dimen...]
    pallas_call x0 -> x1, Pallas kernels: none -> 78.2 us  [window_body(): pl.pallas_call(functools.partial(window_kernel, n_row, n_col), out_shape=...]
    dot_general x8 -> x0, matrix products: 78.1 us -> none  [project(): lax.dot_general(flattened, weight.reshape(-1, weight.shape[-1]), (((1,),...]
    unnamed x2 -> x3, local copies, waits for them, and re-layouts: 0.01 us -> 4.51 us
    add x4 -> x0, other arithmetic: 3.7 us -> none  [gate_sums(): lax.psum_scatter(partial_value.astype(jnp.bfloat16), 'col', scatter_dimen...]
  transfers between devices with their start and end apart: 4 -> 0, of which waited for: 4 -> 0; matrix products, arithmetic and copies ran while one was open for 6% -> 0% of each run, Pallas kernels for 0% -> 0%
where the time goes in v1:
time: 83.6 us; the launch traced here: 83.4 us
  Pallas kernels  78.2 us (94%)
  local copies, waits for them, and re-layouts  4.51 us (5%)
    pallas_call x1, Pallas kernels, window_body(): pl.pallas_call(functools.partial(window_kernel, n_row, n_col), out_shape=...  78.2 us
    unnamed x3, local copies, waits for them, and re-layouts  4.51 us

profile of v1, /device:TPU:0, one launch (start us, length us, event | category | flops | bytes accessed | tf_op | source)
XLA Modules:
  0.0 83.4 jit_solution(17229041635612666836)
XLA Ops:
  0.6 78.2 %shard_map.85 = (bf16[2,64,256]{2,1,0:T(8,128)(2,1)}, bf16[2,64,256]{2,1,0:T(8,128)(2,1)}, f32[2,64,256]{2,1,0:T(8,128)}) custom-call(bf16[2,64,2048]{2,1,0:T(8,128)(2,1)} %inputs.1, bf16[2,4,1024,2048]{3,2,1,0:T(8,128)(2,1)} %w_input.1, bf16[2,4,1024,2048]{3,2,1,0:T(8,128)(2,1)} %w_recur.1, f32[2,4,1024]{2,1,0:T(4,128)} %gate_bias.1, ...), custom_call_target="tpu_custom_call" | custom-call | tf_op jit(solution)/shard_map/pallas_call | solution.py:321
  78.9 1.5 %copy.12 = bf16[2,64,256]{2,1,0:T(8,128)(2,1)} copy(bf16[2,64,256]{2,1,0:T(8,128)(2,1)} %get-tuple-element.6) | data formatting | bytes 131072
  80.3 1.5 %copy.13 = bf16[2,64,256]{2,1,0:T(8,128)(2,1)} copy(bf16[2,64,256]{2,1,0:T(8,128)(2,1)} %get-tuple-element.7) | data formatting | bytes 131072
  81.8 1.6 %copy.14 = f32[2,64,256]{2,1,0:T(8,128)} copy(f32[2,64,256]{2,1,0:T(8,128)} %get-tuple-element.8) | data formatting | bytes 262144

commit v2 on v1

--- a/solution.py
+++ b/solution.py
@@ -83,9 +83,10 @@
 
 def window_kernel(
     n_row, n_col,
-    inputs, w_input, w_recur, gate_bias, hidden_init, cell_init,
-    top_hidden, final_hidden, final_cell,
-    first, second, third, sums, sent, arrived, columns,
+    inputs_in, w_input, w_recur, gate_bias_in, hidden_init_in, cell_init_in,
+    hiddens, cells,
+    inputs, gate_bias, hidden_init, cell_init,
+    first, second, third, sums, sent, arrived, columns, small_sem,
     first_sem, first_again_sem, second_sem, third_sem,
     part_send, part_recv, block_send, block_recv,
 ):
@@ -151,8 +152,8 @@
 
     def product(left, buffer, k):
         return lax.dot_general(
-            left, buffer[k], (((1,), (1,)), ((), ())), preferred_element_type=jnp.float32
-        )
+            buffer[k], left, (((1,), (1,)), ((), ())), preferred_element_type=jnp.float32
+        ).T
 
     def send_part(which, i):
         return pltpu.make_async_remote_copy(
@@ -164,12 +165,10 @@
             device_id_type=MESH,
         )
 
-    def finish(which, held, buffer, i, before=None):
+    def finish(which, held, buffer, i):
         left = vectors(held)
         totals = []
         for g in range(GATES):
-            if before is not None:
-                before(i, g)
             k = i * GATES + g
             totals.append(sums[which, k] + product(left, buffer, k))
 
@@ -204,12 +203,46 @@
             return carried
         lax.fori_loop(begin, end, run, 0)
 
-    for i in range(n_col):
-        for g in range(GATES):
-            load(w_input, 0, first, first_sem, i, g).start()
-    for i in range(n_col):
-        for g in range(GATES):
-            load(w_recur, 0, second, second_sem, i, g).start()
+    small = [
+        pltpu.make_async_copy(source, target, small_sem.at[k])
+        for k, (source, target) in enumerate((
+            (hidden_init_in, hidden_init),
+            (inputs_in, inputs),
+            (gate_bias_in, gate_bias),
+            (cell_init_in, cell_init),
+        ))
+    ]
+    for copy in small:
+        copy.start()
+
+    streams = (
+        (w_input, 0, first, first_sem),
+        (w_recur, 0, second, second_sem),
+        (w_recur, 1, first, first_again_sem),
+        (w_input, 1, third, third_sem),
+    )
+    ahead = min(2, n_col)
+
+    def load_start(which, i):
+        for g in range(GATES):
+            load(*streams[which], i, g).start()
+
+    def load_wait(which, i):
+        for g in range(GATES):
+            load(*streams[which], i, g).wait()
+
+    def next_loads(which, i):
+        @pl.when(i + ahead < n_col)
+        def _():
+            load_start(which, i + ahead)
+
+        if which + 1 < len(streams):
+            @pl.when(i + ahead >= n_col)
+            def _():
+                load_start(which + 1, i + ahead - n_col)
+
+    for i in range(ahead):
+        load_start(0, i)
 
     barrier = pltpu.get_barrier_semaphore()
     targets = [(sibling, col)]
@@ -219,15 +252,20 @@
         pl.semaphore_signal(barrier, inc=1, device_id=target, device_id_type=MESH)
     pl.semaphore_wait(barrier, len(targets))
 
+    small[0].wait()
     for layer in range(2):
         gather_start(layer, hidden_init.at[layer])
         columns[layer, row] = hidden_init[layer]
 
+    for copy in small[1:]:
+        copy.wait()
+
     def input_products(i):
+        load_wait(0, i)
+        next_loads(0, i)
         left = inputs[...].reshape(2 * batch, inputs.shape[2])
         for g in range(GATES):
             k = i * GATES + g
-            load(w_input, 0, first, first_sem, i, g).wait()
             both = product(left, first, k)
             sums[0, k] = both[:batch]
             sums[1, k] = both[batch:]
@@ -240,45 +278,44 @@
     gather_wait(0)
 
     def layer0_step0(i):
-        def before(i, g):
-            load(w_recur, 0, second, second_sem, i, g).wait()
-            load(w_recur, 1, first, first_again_sem, i, g).start()
-
-        finish(0, 0, second, i, before)
+        load_wait(1, i)
+        next_loads(1, i)
+        finish(0, 0, second, i)
 
     loop(0, n_col, layer0_step0)
-    for i in range(n_col):
-        for g in range(GATES):
-            load(w_input, 1, third, third_sem, i, g).start()
     gather_wait(1)
 
     def early_recurrent(i):
+        load_wait(2, i)
+        next_loads(2, i)
         left = vectors(1)
         for g in range(GATES):
             k = i * GATES + g
-            load(w_recur, 1, first, first_again_sem, i, g).wait()
             sums[2, k] = product(left, first, k)
 
     loop(0, half, early_recurrent)
     cell, hidden = cell_step(0, 0, cell_init[0])
     columns[2, row] = hidden
     gather_start(2, columns.at[2, row])
-    final_cell[0] = cell
+    cells[0] = cell
     loop(half, n_col, early_recurrent)
+    for i in range(ahead, n_col):
+        load_start(3, i)
     gather_forward(2)
     gather_wait(2)
 
     loop(0, n_col, lambda i: finish(1, 2, second, i))
 
     def layer1_step0(i):
-        finish(2, 2, third, i, lambda i, g: load(w_input, 1, third, third_sem, i, g).wait())
+        load_wait(3, i)
+        finish(2, 2, third, i)
 
     loop(0, half, layer1_step0)
-    cell, hidden = cell_step(1, 0, final_cell[0])
+    cell, hidden = cell_step(1, 0, cells[0])
     columns[3, row] = hidden
     gather_start(3, columns.at[3, row])
-    final_cell[0] = cell
-    final_hidden[0] = hidden
+    cells[0] = cell
+    hiddens[2] = hidden
     loop(half, n_col, layer1_step0)
     gather_forward(3)
     gather_wait(3)
@@ -293,22 +330,28 @@
     cell, hidden = cell_step(2, 1, cell_init[1])
     columns[4, row] = hidden
     gather_start(4, columns.at[4, row])
-    final_cell[1] = cell
-    top_hidden[0] = hidden
+    cells[1] = cell
+    hiddens[0] = hidden
     loop(half, n_col, late_input)
     gather_forward(4)
     gather_wait(4)
     loop(0, n_col, lambda i: finish(3, 4, first, i))
-    cell, hidden = cell_step(3, 1, final_cell[1])
-    final_cell[1] = cell
-    top_hidden[1] = hidden
-    final_hidden[1] = hidden
+    cell, hidden = cell_step(3, 1, cells[1])
+    cells[1] = cell
+    hiddens[1] = hidden
 
     for which in range(5):
         gather_end(which)
     for which in range(4):
         for i in range(last):
             send_part(which, i).wait_send()
+
+
+def output_kernel(hiddens, cells, top_hidden, final_hidden, final_cell):
+    top_hidden[...] = hiddens[:2]
+    final_hidden[0] = hiddens[2]
+    final_hidden[1] = hiddens[1]
+    final_cell[...] = cells[...]
 
 
 def window_body(n_row, n_col, inputs, w_input, w_recur, gate_bias, hidden_init, cell_init):
@@ -318,16 +361,19 @@
     chips = n_row // 2
     vmem = pl.BlockSpec(memory_space=pltpu.VMEM)
     hbm = pl.BlockSpec(memory_space=pl.ANY)
-    return pl.pallas_call(
+    hiddens, cells = pl.pallas_call(
         functools.partial(window_kernel, n_row, n_col),
         out_shape=(
-            jax.ShapeDtypeStruct((2, batch, unit), jnp.bfloat16),
-            jax.ShapeDtypeStruct((2, batch, unit), jnp.bfloat16),
+            jax.ShapeDtypeStruct((3, batch, unit), jnp.bfloat16),
             jax.ShapeDtypeStruct((2, batch, unit), jnp.float32),
         ),
-        in_specs=[vmem, hbm, hbm, vmem, vmem, vmem],
-        out_specs=(vmem, vmem, vmem),
+        in_specs=[hbm] * 6,
+        out_specs=(vmem, vmem),
         scratch_shapes=[
+            pltpu.VMEM(inputs.shape, inputs.dtype),
+            pltpu.VMEM(gate_bias.shape, gate_bias.dtype),
+            pltpu.VMEM(hidden_init.shape, hidden_init.dtype),
+            pltpu.VMEM(cell_init.shape, cell_init.dtype),
             pltpu.VMEM((chunks, unit, depth), jnp.bfloat16),
             pltpu.VMEM((chunks, unit, depth), jnp.bfloat16),
             pltpu.VMEM((chunks, unit, depth), jnp.bfloat16),
@@ -335,6 +381,7 @@
             pltpu.VMEM((4, n_col - 1, GATES, batch, unit), jnp.bfloat16),
             pltpu.VMEM((4, n_col - 1, GATES, batch, unit), jnp.bfloat16),
             pltpu.VMEM((5, n_row, batch, unit), jnp.bfloat16),
+            pltpu.SemaphoreType.DMA((4,)),
             pltpu.SemaphoreType.DMA((chunks,)),
             pltpu.SemaphoreType.DMA((chunks,)),
             pltpu.SemaphoreType.DMA((chunks,)),
@@ -348,6 +395,16 @@
             collective_id=0, has_side_effects=True, vmem_limit_bytes=LOCAL_VMEM
         ),
     )(inputs, w_input, w_recur, gate_bias, hidden_init, cell_init)
+    return pl.pallas_call(
+        output_kernel,
+        out_shape=(
+            jax.ShapeDtypeStruct((2, batch, unit), jnp.bfloat16),
+            jax.ShapeDtypeStruct((2, batch, unit), jnp.bfloat16),
+            jax.ShapeDtypeStruct((2, batch, unit), jnp.float32),
+        ),
+        in_specs=[vmem, vmem],
+        out_specs=(vmem, vmem, vmem),
+    )(hiddens, cells)
 
 
 def solution(mesh):

time: 83.6 us -> 66.1 us (0.79)
  Pallas kernels: 78.2 us -> 65.3 us
  local copies, waits for them, and re-layouts: 4.51 us -> 0 us
    pallas_call x1, Pallas kernels: 78.2 us -> 63.7 us  [window_body(): pl.pallas_call(functools.partial(window_kernel, n_row, n_col), out_shape=...]
    unnamed x3 -> x0, local copies, waits for them, and re-layouts: 4.51 us -> none
    pallas_call x0 -> x1, Pallas kernels: none -> 1.66 us  [window_body(): pl.pallas_call(output_kernel, out_shape=(jax.ShapeDtypeStruct((2, batch,...]
where the time goes in v2:
time: 66.1 us; the launch traced here: 66 us
  Pallas kernels  65.3 us (99%)
    pallas_call x1, Pallas kernels, window_body(): pl.pallas_call(functools.partial(window_kernel, n_row, n_col), out_shape=...  63.7 us
    pallas_call x1, Pallas kernels, window_body(): pl.pallas_call(output_kernel, out_shape=(jax.ShapeDtypeStruct((2, batch,...  1.66 us

profile of v2, /device:TPU:0, one launch (start us, length us, event | category | flops | bytes accessed | tf_op | source)
XLA Modules:
  0.0 66.0 jit_solution(2452712370564395655)
XLA Ops:
  0.6 63.7 %shard_map.85 = (bf16[3,64,256]{2,1,0:T(8,128)(2,1)}, f32[2,64,256]{2,1,0:T(8,128)}) custom-call(bf16[2,64,2048]{2,1,0:T(8,128)(2,1)} %inputs_in.1, bf16[2,4,1024,2048]{3,2,1,0:T(8,128)(2,1)} %w_input.1, bf16[2,4,1024,2048]{3,2,1,0:T(8,128)(2,1)} %w_recur.1, f32[2,4,1024]{2,1,0:T(4,128)} %gate_bias_in.1, bf16[2,64,256]{2,1,0:T(8,128)(2,1)} %hidden_init_in.1, ...), custom_call_target="tpu_custom_call" | custom-call | tf_op jit(solution)/shard_map/pallas_call | solution.py:364
  64.3 1.7 %shard_map.86 = (bf16[2,64,256]{2,1,0:T(8,128)(2,1)}, bf16[2,64,256]{2,1,0:T(8,128)(2,1)}, f32[2,64,256]{2,1,0:T(8,128)}) custom-call(bf16[3,64,256]{2,1,0:T(8,128)(2,1)} %get-tuple-element.5.hiddens, f32[2,64,256]{2,1,0:T(8,128)} %get-tuple-element.6.cells), custom_call_target="tpu_custom_call" | custom-call | tf_op jit(solution)/shard_map/pallas_call | solution.py:398

commit v3 on v2

--- a/solution.py
+++ b/solution.py
@@ -318,22 +318,22 @@
     hiddens[2] = hidden
     loop(half, n_col, layer1_step0)
     gather_forward(3)
-    gather_wait(3)
-
-    def late_input(i):
-        left = vectors(3)
-        for g in range(GATES):
-            k = i * GATES + g
-            sums[3, k] = product(left, third, k)
-
-    loop(0, half, late_input)
     cell, hidden = cell_step(2, 1, cell_init[1])
     columns[4, row] = hidden
     gather_start(4, columns.at[4, row])
     cells[1] = cell
     hiddens[0] = hidden
-    loop(half, n_col, late_input)
+    gather_wait(3)
+
+    def late_input(i):
+        left = vectors(3)
+        for g in range(GATES):
+            k = i * GATES + g
+            sums[3, k] = product(left, third, k)
+
+    loop(0, last, late_input)
     gather_forward(4)
+    loop(last, n_col, late_input)
     gather_wait(4)
     loop(0, n_col, lambda i: finish(3, 4, first, i))
     cell, hidden = cell_step(3, 1, cells[1])

time: 66.1 us -> 64.6 us (0.977)
  Pallas kernels: 65.3 us -> 63.8 us
    pallas_call x1, Pallas kernels: 63.7 us -> 62.1 us  [window_body(): pl.pallas_call(functools.partial(window_kernel, n_row, n_col), out_shape=...]
where the time goes in v3:
time: 64.6 us; the launch traced here: 64.4 us
  Pallas kernels  63.8 us (99%)
    pallas_call x1, Pallas kernels, window_body(): pl.pallas_call(functools.partial(window_kernel, n_row, n_col), out_shape=...  62.1 us
    pallas_call x1, Pallas kernels, window_body(): pl.pallas_call(output_kernel, out_shape=(jax.ShapeDtypeStruct((2, batch,...  1.66 us

profile of v3, /device:TPU:0, one launch (start us, length us, event | category | flops | bytes accessed | tf_op | source)
XLA Modules:
  0.0 64.4 jit_solution(4813792050597798121)
XLA Ops:
  0.6 62.1 %shard_map.85 = (bf16[3,64,256]{2,1,0:T(8,128)(2,1)}, f32[2,64,256]{2,1,0:T(8,128)}) custom-call(bf16[2,64,2048]{2,1,0:T(8,128)(2,1)} %inputs_in.1, bf16[2,4,1024,2048]{3,2,1,0:T(8,128)(2,1)} %w_input.1, bf16[2,4,1024,2048]{3,2,1,0:T(8,128)(2,1)} %w_recur.1, f32[2,4,1024]{2,1,0:T(4,128)} %gate_bias_in.1, bf16[2,64,256]{2,1,0:T(8,128)(2,1)} %hidden_init_in.1, ...), custom_call_target="tpu_custom_call" | custom-call | tf_op jit(solution)/shard_map/pallas_call | solution.py:364
  62.8 1.7 %shard_map.86 = (bf16[2,64,256]{2,1,0:T(8,128)(2,1)}, bf16[2,64,256]{2,1,0:T(8,128)(2,1)}, f32[2,64,256]{2,1,0:T(8,128)}) custom-call(bf16[3,64,256]{2,1,0:T(8,128)(2,1)} %get-tuple-element.5.hiddens, f32[2,64,256]{2,1,0:T(8,128)} %get-tuple-element.6.cells), custom_call_target="tpu_custom_call" | custom-call | tf_op jit(solution)/shard_map/pallas_call | solution.py:398
